TPU v7x, 32 devices: a whole 2x2x4 slice. The times are simulated.
32 devices in a mesh: rep: 4 (over y, x), shard: 8 (over z, core).
Axes of the slice: x: 2, y: 2, z: 4, core: 2. Of those that a mesh axis runs over, the one named last changes fastest.
Arguments:
- tokens: bfloat16 [4096, 768], P(('rep', 'shard')), may hold values from -6 to 6
- segment_ids: int32 [32, 128], P(('rep', 'shard')), may hold values from 0 to 3, never falling along the last dimension, each value on 1 to 64 neighbouring positions
- first_gain: bfloat16 [768], P('shard'), may hold values from 0.5 to 1.5
- first_shift: bfloat16 [768], P('shard'), may hold values from -3 to 3
- qkv_weight: bfloat16 [768, 2304], P('shard'), may hold values from -3 to 3, as said below
- qv_bias: bfloat16 [2, 768], P(None, 'shard'), may hold values from -3 to 3
- proj_weight: bfloat16 [768, 768], P('shard'), may hold values from -0.625 to 0.625
- proj_bias: bfloat16 [768], P('shard'), may hold values from -3 to 3
- second_gain: bfloat16 [768], P('shard'), may hold values from 0.5 to 1.5
- second_shift: bfloat16 [768], P('shard'), may hold values from -3 to 3
- fc_weight: bfloat16 [768, 3072], P('shard'), may hold values from -0.21875 to 0.21875
- fc_bias: bfloat16 [3072], P('shard'), may hold values from -3 to 3
- out_weight: bfloat16 [3072, 768], P('shard'), may hold values from -0.109375 to 0.109375
- out_bias: bfloat16 [768], P('shard'), may hold values from -3 to 3
- cotangent: bfloat16 [4096, 768], P(('rep', 'shard')), may hold values from -6 to 6
Outputs:
- block_output: bfloat16 [4096, 768], P(('rep', 'shard'))
- grad_tokens: float32 [4096, 768], P(('rep', 'shard'))
- grad_first_gain: float32 [768], P('shard')
- grad_first_shift: float32 [768], P('shard')
- grad_qkv_weight: float32 [768, 2304], P('shard')
- grad_qv_bias: float32 [2, 768], P(None, 'shard')
- grad_proj_weight: float32 [768, 768], P('shard')
- grad_proj_bias: float32 [768], P('shard')
- grad_second_gain: float32 [768], P('shard')
- grad_second_shift: float32 [768], P('shard')
- grad_fc_weight: float32 [768, 3072], P('shard')
- grad_fc_bias: float32 [3072], P('shard')
- grad_out_weight: float32 [3072, 768], P('shard')
- grad_out_bias: float32 [768], P('shard')
Inputs may be any that keep to these rules, and one draw needn't show every extreme that they name: `segment_ids`: each row holds 4 runs of equal numbers in rising order, each run 1 to 64 long, one of them exactly 64. `qkv_weight`: columns 0 to 767 project to queries, the next 768 columns to keys, the last 768 columns to values.
All inputs are finite; a program needn't handle non-finite values.
Results may differ from a plain program's by a relative error of at most 0.011.
Values may be sent and summed in bfloat16 or wider, within the bound.
A program may use at most 128 MiB of HBM per device.

v0:
```python
import math
import jax
import jax.numpy as jnp
from jax import lax
from jax.sharding import PartitionSpec as P

D = 768
HEADS = 12
HD = 64
EPSILON = 1e-05


def layer_norm(field, norm_gain, norm_shift):
    center = field - jnp.mean(field, axis=-1, keepdims=True)
    spread = jnp.mean(center * center, axis=-1, keepdims=True)
    return center * lax.rsqrt(spread + EPSILON) * norm_gain + norm_shift


def gelu_tanh(field):
    return jax.nn.gelu(field, approximate=True)


def head_split(matrix):
    return matrix.reshape(matrix.shape[0], HEADS, HD)


def masked_scores(query, keys, segments):
    rows = query.shape[0]
    scores = jnp.einsum(
        "qhd,khd->hqk", head_split(query), head_split(keys), preferred_element_type=jnp.float32
    ) * (1.0 / math.sqrt(HD))
    position = lax.iota(jnp.int32, rows)
    allowed = (segments[:, None] == segments[None, :]) & (position[None, :] <= position[:, None])
    return jnp.where(allowed[None], scores, -1e30)


def attend_forward(query, keys, values, segments):
    rows = query.shape[0]
    scores = masked_scores(query, keys, segments)
    row_max = jnp.max(scores, axis=-1, keepdims=True)
    row_total = jnp.sum(jnp.exp(scores - row_max), axis=-1, keepdims=True)
    logsum = row_max + jnp.log(row_total)
    probs = jnp.exp(scores - logsum).astype(jnp.bfloat16)
    attended = jnp.einsum(
        "hqk,khd->qhd", probs, head_split(values), preferred_element_type=jnp.float32
    )
    return (attended.reshape(rows, D).astype(jnp.bfloat16), logsum)


def attend_backward(query, keys, values, segments, attended, logsum, grad_attended):
    rows = query.shape[0]
    scores = masked_scores(query, keys, segments)
    weights = jnp.exp(scores - logsum)
    grad_heads = head_split(grad_attended)
    grad_values = jnp.einsum(
        "hqk,qhd->khd", weights.astype(jnp.bfloat16), grad_heads, preferred_element_type=jnp.float32
    )
    grad_probs = jnp.einsum(
        "qhd,khd->hqk", grad_heads, head_split(values), preferred_element_type=jnp.float32
    )
    delta = jnp.einsum(
        "qhd,qhd->hq", grad_heads, head_split(attended), preferred_element_type=jnp.float32
    )
    grad_scores = (weights * (grad_probs - delta[..., None]) * (1.0 / math.sqrt(HD))).astype(
        jnp.bfloat16
    )
    grad_query = jnp.einsum(
        "hqk,khd->qhd", grad_scores, head_split(keys), preferred_element_type=jnp.float32
    )
    grad_keys = jnp.einsum(
        "hqk,qhd->khd", grad_scores, head_split(query), preferred_element_type=jnp.float32
    )
    return (grad_query.reshape(rows, D), grad_keys.reshape(rows, D), grad_values.reshape(rows, D))


def per_device(
    tokens,
    segment_ids,
    first_gain,
    first_shift,
    qkv_weight,
    qv_bias,
    proj_weight,
    proj_bias,
    second_gain,
    second_shift,
    fc_weight,
    fc_bias,
    out_weight,
    out_bias,
    cotangent,
):
    low = jnp.bfloat16
    segments = segment_ids[0]
    own_rows = tokens.shape[0]
    shards = lax.axis_size("shard")
    reps = lax.axis_size("rep")
    factor = 1.0 / math.sqrt(own_rows * reps * shards)
    small = jnp.stack(
        [
            first_gain,
            first_shift,
            qv_bias[0],
            qv_bias[1],
            proj_bias,
            second_gain,
            second_shift,
            out_bias,
        ]
    )
    small_full = lax.all_gather(small, "shard", axis=1, tiled=True).astype(jnp.float32)
    gain_one, shift_one, q_bias, v_bias, proj_bias_full, gain_two, shift_two, out_bias_full = (
        small_full[i] for i in range(8)
    )
    qkv_full = lax.all_gather(qkv_weight, "shard", axis=0, tiled=True)
    proj_full = lax.all_gather(proj_weight, "shard", axis=0, tiled=True)
    fc_cols = lax.all_to_all(fc_weight, "shard", split_axis=1, concat_axis=0, tiled=True)
    cot_all = lax.all_gather(cotangent, "shard", axis=0, tiled=True)
    inputs = tokens.astype(jnp.float32)
    normed_f, first_back = jax.vjp(layer_norm, inputs, gain_one, shift_one)
    normed_first = normed_f.astype(low)
    projected = jnp.dot(normed_first, qkv_full, preferred_element_type=jnp.float32)
    query = (projected[:, :D] + q_bias).astype(low)
    keys = projected[:, D : 2 * D].astype(low)
    values = (projected[:, 2 * D :] + v_bias).astype(low)
    attended, logsum = attend_forward(query, keys, values, segments)
    residual = (
        inputs + jnp.dot(attended, proj_full, preferred_element_type=jnp.float32) + proj_bias_full
    )
    cot_f = cotangent.astype(jnp.float32)
    term_out_bias = jnp.sum(cot_f, axis=0) * factor
    normed_s, second_back = jax.vjp(layer_norm, residual, gain_two, shift_two)
    normed_second = normed_s.astype(low)
    normed_all = lax.all_gather(normed_second, "shard", axis=0, tiled=True)
    pre_act = jnp.dot(normed_all, fc_cols, preferred_element_type=jnp.float32) + fc_bias.astype(
        jnp.float32
    )
    activated, gelu_back = jax.vjp(gelu_tanh, pre_act)
    hidden = activated.astype(low)
    grad_hidden = jnp.dot(cot_all, out_weight.T, preferred_element_type=jnp.float32)
    (grad_pre,) = gelu_back(grad_hidden)
    grad_pre_low = grad_pre.astype(low)
    term_fc_bias = jnp.sum(grad_pre, axis=0) * factor
    grad_normed_part = jnp.dot(grad_pre_low, fc_cols.T, preferred_element_type=jnp.float32).astype(
        low
    )
    grad_normed_second = lax.psum_scatter(
        grad_normed_part, "shard", scatter_dimension=0, tiled=True
    ).astype(jnp.float32)
    out_part = jnp.dot(hidden, out_weight, preferred_element_type=jnp.float32).astype(low)
    out_sum = lax.psum_scatter(out_part, "shard", scatter_dimension=0, tiled=True).astype(
        jnp.float32
    )
    result = (residual + out_sum + out_bias_full).astype(low)
    term_out_weight = (
        jnp.dot(hidden.T, cot_all, preferred_element_type=jnp.float32) * factor
    ).astype(low)
    term_fc_weight = (
        jnp.dot(normed_all.T, grad_pre_low, preferred_element_type=jnp.float32) * factor
    ).astype(low)
    out_piece = lax.psum_scatter(term_out_weight, "rep", scatter_dimension=0, tiled=True)
    out_grad = lax.all_gather(out_piece, "rep", axis=0, tiled=True).astype(jnp.float32)
    fc_own = D // (shards * reps)
    fc_rows = term_fc_weight.reshape(shards, reps, fc_own, -1).swapaxes(0, 1).reshape(D, -1)
    fc_piece = lax.psum_scatter(fc_rows, "rep", scatter_dimension=0, tiled=True)
    fc_piece = lax.all_to_all(fc_piece, "shard", split_axis=0, concat_axis=1, tiled=True)
    fc_grad = lax.all_gather(fc_piece, "rep", axis=0, tiled=True).astype(jnp.float32)
    grad_from_norm, second_gain_sum, second_shift_sum = second_back(grad_normed_second)
    grad_residual = cot_f + grad_from_norm
    grad_residual_low = grad_residual.astype(low)
    term_proj_bias = jnp.sum(grad_residual, axis=0) * factor
    term_proj_weight = (
        jnp.dot(attended.T, grad_residual_low, preferred_element_type=jnp.float32) * factor
    ).astype(low)
    grad_attended = jnp.dot(
        grad_residual_low, proj_full.T, preferred_element_type=jnp.float32
    ).astype(low)
    grad_query, grad_keys, grad_values = attend_backward(
        query, keys, values, segments, attended, logsum, grad_attended
    )
    grad_projected = jnp.concatenate([grad_query, grad_keys, grad_values], axis=1).astype(low)
    term_qkv_weight = (
        jnp.dot(normed_first.T, grad_projected, preferred_element_type=jnp.float32) * factor
    ).astype(low)
    grad_normed_first = jnp.dot(grad_projected, qkv_full.T, preferred_element_type=jnp.float32)
    grad_input_norm, first_gain_sum, first_shift_sum = first_back(grad_normed_first)
    grad_inputs = grad_residual + grad_input_norm
    proj_share = lax.psum_scatter(term_proj_weight, "shard", scatter_dimension=0, tiled=True)
    qkv_share = lax.psum_scatter(term_qkv_weight, "shard", scatter_dimension=0, tiled=True)
    proj_piece = lax.psum_scatter(proj_share, "rep", scatter_dimension=0, tiled=True)
    qkv_piece = lax.psum_scatter(qkv_share, "rep", scatter_dimension=0, tiled=True)
    proj_grad = lax.all_gather(proj_piece, "rep", axis=0, tiled=True).astype(jnp.float32)
    qkv_grad = lax.all_gather(qkv_piece, "rep", axis=0, tiled=True).astype(jnp.float32)
    terms = jnp.stack(
        [
            first_gain_sum * factor,
            first_shift_sum * factor,
            jnp.sum(grad_query, axis=0) * factor,
            jnp.sum(grad_values, axis=0) * factor,
            term_proj_bias,
            second_gain_sum * factor,
            second_shift_sum * factor,
            term_out_bias,
        ]
    )
    sums, fc_bias_grad = lax.psum(
        (lax.psum_scatter(terms, "shard", scatter_dimension=1, tiled=True), term_fc_bias), "rep"
    )
    return (
        result,
        grad_inputs,
        sums[0],
        sums[1],
        qkv_grad,
        sums[2:4],
        proj_grad,
        sums[4],
        sums[5],
        sums[6],
        fc_grad,
        fc_bias_grad,
        out_grad,
        sums[7],
    )


def solution(mesh):
    return jax.shard_map(
        per_device,
        mesh=mesh,
        in_specs=(
            P(("rep", "shard"), None),
            P(("rep", "shard"), None),
            P("shard"),
            P("shard"),
            P("shard", None),
            P(None, "shard"),
            P("shard", None),
            P("shard"),
            P("shard"),
            P("shard"),
            P("shard", None),
            P("shard"),
            P("shard", None),
            P("shard"),
            P(("rep", "shard"), None),
        ),
        out_specs=(
            P(("rep", "shard"), None),
            P(("rep", "shard"), None),
            P("shard"),
            P("shard"),
            P("shard", None),
            P(None, "shard"),
            P("shard", None),
            P("shard"),
            P("shard"),
            P("shard"),
            P("shard", None),
            P("shard"),
            P("shard", None),
            P("shard"),
        ),
        check_vma=False,
    )
```

profile of v0, /device:TPU:0, one launch (start us, length us, event | category | flops | bytes accessed | tf_op | source)
XLA Modules:
  0.0 454.6 jit_solution(13503436207554731537)
XLA Ops:
  12.4 14.4 %all-gather = bf16[8,96,8]{1,2,0:T(8,128)(2,1)S(1)} all-gather(bf16[1,96,8]{1,2,0:T(8,128)(2,1)S(1)} %bitcast.120), channel_id=1, replica_groups=mesh['rep'=4,'shard'=8] {'shard'}, dimensions={0}, use_global_device_ids=true | all-gather | bytes 13824 | tf_op jit(solution)/shard_map/all_gather | solution.py:111
  27.9 26.1 %all-gather.6.cloned.1.call-done = bf16[768,2304]{1,0:T(8,128)(2,1)} async-done(((bf16[96,2304]{1,0:T(8,128)(2,1)}), bf16[768,2304]{1,0:T(8,128)(2,1)}) %all-gather.6.cloned.1.call-update) | async-done | bytes 3538960 | tf_op jit(solution)/shard_map/all_gather | solution.py:115
  58.2 19.0 %all-gather.8.cloned.1.call-done = bf16[768,768]{1,0:T(8,128)(2,1)} async-done(((bf16[96,768]{1,0:T(8,128)(2,1)}), bf16[768,768]{1,0:T(8,128)(2,1)}) %all-gather.8.cloned.1.call-update) | async-done | bytes 1179664 | tf_op jit(solution)/shard_map/all_gather | solution.py:116
  80.9 3.5 all-to-all-start
  84.5 30.8 %all-gather.12.cloned.1.call-done = bf16[1024,768]{1,0:T(8,128)(2,1)} async-done(((bf16[128,768]{1,0:T(8,128)(2,1)}), bf16[1024,768]{1,0:T(8,128)(2,1)}) %all-gather.12.cloned.1.call-update) | async-done | bytes 1572880 | tf_op jit(solution)/shard_map/all_gather | solution.py:118
  115.3 3.6 fusion.57
  118.9 22.4 %all-gather.10.cloned.1.call-done = bf16[1024,768]{1,0:T(8,128)(2,1)} async-done(((bf16[128,768]{1,0:T(8,128)(2,1)}), bf16[1024,768]{1,0:T(8,128)(2,1)}) %all-gather.10.cloned.1.call-update) | async-done | bytes 1572880 | tf_op jit(solution)/shard_map/all_gather | solution.py:134
  141.3 5.5 %fusion.50 = (f32[384]{0:T(512)}, bf16[1024,384]{1,0:T(8,128)(2,1)S(1)}, f32[1024,384]{1,0:T(8,128)}) fusion(f32[1024,384]{1,0:T(8,128)} %fusion.57, f32[384]{0:T(512)S(1)} %convert_element_type.105, bf16[1024,768]{1,0:T(8,128)(2,1)} %all-gather.10.cloned.1.call-done, bf16[768,384]{1,0:T(8,128)(2,1)S(1)} %bitcast.112), kind=kOutput, calls=%fused_computation.118 | convolution fusion | flops 612630144 | bytes 6097920 | tf_op jit(solution)/shard_map/dot_general | solution.py:135
  150.0 3.8 convolution_convert_fusion.1
  153.9 30.1 %reduce-scatter.18.cloned.1.call-done = bf16[128,768]{1,0:T(8,128)(2,1)} async-done(((bf16[1024,768]{1,0:T(8,128)(2,1)}), bf16[128,768]{1,0:T(8,128)(2,1)}) %reduce-scatter.18.cloned.1.call-update) | async-done | bytes 196624 | tf_op jit(solution)/shard_map/reduce_scatter | solution.py:147
  187.5 30.8 %reduce-scatter.16.cloned.1.call-done = bf16[128,768]{1,0:T(8,128)(2,1)} async-done(((bf16[1024,768]{1,0:T(8,128)(2,1)}), bf16[128,768]{1,0:T(8,128)(2,1)}) %reduce-scatter.16.cloned.1.call-update) | async-done | bytes 196624 | tf_op jit(solution)/shard_map/reduce_scatter | solution.py:151
  243.1 10.2 %reduce-scatter.22.cloned.1.call-done = bf16[96,768]{1,0:T(8,128)(2,1)} async-done(((bf16[768,768]{1,0:T(8,128)(2,1)}), bf16[96,768]{1,0:T(8,128)(2,1)}) %reduce-scatter.22.cloned.1.call-update) | async-done | bytes 147472 | tf_op jit(solution)/shard_map/reduce_scatter | solution.py:188
  253.3 26.6 %reduce-scatter.24.cloned.1.call-done = bf16[192,384]{1,0:T(8,128)(2,1)} async-done(((bf16[768,384]{1,0:T(8,128)(2,1)}), bf16[192,384]{1,0:T(8,128)(2,1)}) %reduce-scatter.24.cloned.1.call-update) | async-done | bytes 147472 | tf_op jit(solution)/shard_map/reduce_scatter | solution.py:165
  279.9 4.6 %all-to-all-start.1 = ((bf16[8,24,384]{2,1,0:T(8,128)(2,1)}), bf16[8,24,384]{2,1,0:T(8,128)(2,1)S(1)}, u32[]{:S(2)}, u32[]{:S(2)}) async-start(bf16[8,24,384]{2,1,0:T(8,128)(2,1)} %bitcast.117), calls=%async_computation.6 | async-start | bytes 294912 | tf_op jit(solution)/shard_map/all_to_all | solution.py:166
  284.5 41.6 %reduce-scatter.20.cloned.1.call-done = bf16[96,2304]{1,0:T(8,128)(2,1)} async-done(((bf16[768,2304]{1,0:T(8,128)(2,1)}), bf16[96,2304]{1,0:T(8,128)(2,1)}) %reduce-scatter.20.cloned.1.call-update) | async-done | bytes 442384 | tf_op jit(solution)/shard_map/reduce_scatter | solution.py:189
  326.2 26.9 %reduce-scatter.26.cloned.1.call-done = bf16[96,768]{1,0:T(8,128)(2,1)} async-done(((bf16[384,768]{1,0:T(8,128)(2,1)}), bf16[96,768]{1,0:T(8,128)(2,1)}) %reduce-scatter.26.cloned.1.call-update) | async-done | bytes 147472 | tf_op jit(solution)/shard_map/reduce_scatter | solution.py:161
  353.0 10.2 %all_gather.35 = bf16[384,768]{1,0:T(8,128)(2,1)S(1)} all-gather(bf16[96,768]{1,0:T(8,128)(2,1)} %reduce-scatter.26.cloned.1.call-done), channel_id=1, replica_groups=mesh['rep'=4,'shard'=8] {'rep'}, dimensions={0}, use_global_device_ids=true | all-gather | bytes 737280 | tf_op jit(solution)/shard_map/all_gather | solution.py:162
  364.4 10.5 %all_gather.34 = bf16[96,3072]{1,0:T(8,128)(2,1)S(1)} all-gather(bf16[24,3072]{1,0:T(8,128)(2,1)S(1)} %bitcast.116), channel_id=1, replica_groups=mesh['rep'=4,'shard'=8] {'rep'}, dimensions={0}, use_global_device_ids=true | all-gather | bytes 737280 | tf_op jit(solution)/shard_map/all_gather | solution.py:167
  376.9 9.2 %reduce-scatter.28.cloned.1.call-done = f32[96,8]{1,0:T(8,128)} async-done(((f32[768,8]{1,0:T(8,128)}), f32[96,8]{1,0:T(8,128)}) %reduce-scatter.28.cloned.1.call-update) | async-done | bytes 3088
  387.0 10.5 %all-reduce.2 = (f32[8,96]{1,0:T(8,128)S(1)}, f32[384]{0:T(512)}) all-reduce(f32[8,96]{1,0:T(8,128)S(1)} %copy.93, f32[384]{0:T(512)S(1)} %broadcast_multiply_fusion.8), channel_id=1, replica_groups=mesh['rep'=4,'shard'=8] {'rep'}, use_global_device_ids=true, to_apply=%region_21.22 | all-reduce | flops 1152 | bytes 9216 | tf_op jit(solution)/shard_map/psum | solution.py:206
  398.6 11.6 %reduce-scatter.32.cloned.1.call-done = bf16[24,768]{1,0:T(8,128)(2,1)} async-done(((bf16[96,768]{1,0:T(8,128)(2,1)}), bf16[24,768]{1,0:T(8,128)(2,1)}) %reduce-scatter.32.cloned.1.call-update) | async-done | bytes 36880
  410.2 8.5 %all_gather.33 = bf16[96,768]{1,0:T(8,128)(2,1)S(1)} all-gather(bf16[24,768]{1,0:T(8,128)(2,1)} %reduce-scatter.32.cloned.1.call-done), channel_id=1, replica_groups=mesh['rep'=4,'shard'=8] {'rep'}, dimensions={0}, use_global_device_ids=true | all-gather | bytes 184320 | tf_op jit(solution)/shard_map/all_gather | solution.py:192
  419.5 17.9 %reduce-scatter.30.cloned.1.call-done = bf16[24,2304]{1,0:T(8,128)(2,1)} async-done(((bf16[96,2304]{1,0:T(8,128)(2,1)}), bf16[24,2304]{1,0:T(8,128)(2,1)}) %reduce-scatter.30.cloned.1.call-update) | async-done | bytes 110608
  437.4 9.7 %all_gather.32 = bf16[96,2304]{1,0:T(8,128)(2,1)S(1)} all-gather(bf16[24,2304]{1,0:T(8,128)(2,1)} %reduce-scatter.30.cloned.1.call-done), channel_id=1, replica_groups=mesh['rep'=4,'shard'=8] {'rep'}, dimensions={0}, use_global_device_ids=true | all-gather | bytes 552960 | tf_op jit(solution)/shard_map/all_gather | solution.py:193
  (151 shorter events, 52.1 us)
Async XLA Ops:
  7.2 108.1 %copy-start = (bf16[384,768]{1,0:T(8,128)(2,1)S(1)}, bf16[384,768]{1,0:T(8,128)(2,1)}, u32[]{:S(2)}) copy-start(bf16[384,768]{1,0:T(8,128)(2,1)} %param.27) | copy-start | bytes 1769476
  7.2 46.8 %all-gather.6.cloned.1.call-start = ((), (), s32[]{:S(2)}) async-start(), calls=%async_computation.11 | async-start | bytes 3981312 | tf_op jit(solution)/shard_map/all_gather | solution.py:115
  7.9 69.2 %all-gather.8.cloned.1.call-start = ((), (), s32[]{:S(2)}) async-start(), calls=%async_computation.12 | async-start | bytes 1327104 | tf_op jit(solution)/shard_map/all_gather | solution.py:116
  8.7 106.6 %all-gather.12.cloned.1.call-start = ((), (), s32[]{:S(2)}) async-start(), calls=%async_computation.15 | async-start | bytes 1769472 | tf_op jit(solution)/shard_map/all_gather | solution.py:118
  9.4 131.9 %all-gather.10.cloned.1.call-start = ((), (), s32[]{:S(2)}) async-start(), calls=%async_computation.13 | async-start | bytes 1769472 | tf_op jit(solution)/shard_map/all_gather | solution.py:134
  10.5 46.3 %copy-start.10 = (f32[128]{0:T(128)}, f32[128]{0:T(128)S(1)}, u32[]{:S(2)}) copy-start(f32[128]{0:T(128)S(1)} %broadcast_multiply_fusion.10) | copy-start | bytes 1540
  11.6 45.1 %copy-start.20 = (f32[128]{0:T(128)}, f32[128]{0:T(128)S(1)}, u32[]{:S(2)}) copy-start(f32[128]{0:T(128)S(1)} %fusion.26) | copy-start | bytes 1540
  27.9 28.9 %copy-start.16 = (f32[128]{0:T(128)}, f32[128]{0:T(128)S(1)}, u32[]{:S(2)}) copy-start(f32[128]{0:T(128)S(1)} %fusion.40) | copy-start | bytes 1540
  57.4 19.7 %copy-start.1 = (bf16[128,768]{1,0:T(8,128)(2,1)S(1)}, bf16[128,768]{1,0:T(8,128)(2,1)}, u32[]{:S(2)}) copy-start(bf16[128,768]{1,0:T(8,128)(2,1)} %param.15) | copy-start | bytes 589828
  79.1 5.3 %copy-start.19 = (bf16[384]{0:T(512)(128)(2,1)S(1)}, bf16[384]{0:T(512)(128)(2,1)}, u32[]{:S(2)}) copy-start(bf16[384]{0:T(512)(128)(2,1)} %param.26) | copy-start | bytes 2308
  80.9 38.0 %all-to-all-start = ((bf16[96,8,384]{2,0,1:T(8,128)(2,1)}), bf16[96,8,384]{2,0,1:T(8,128)(2,1)S(1)}, u32[]{:S(2)}, u32[]{:S(2)}) async-start(bf16[96,8,384]{2,0,1:T(8,128)(2,1)} %bitcast.91), calls=%async_computation | async-start | bytes 1179648 | tf_op jit(solution)/shard_map/all_to_all | solution.py:117
  84.4 99.5 %reduce-scatter.18.cloned.1.call-start = ((), (), s32[]{:S(2)}) async-start(), calls=%async_computation.16 | async-start | bytes 1769472 | tf_op jit(solution)/shard_map/reduce_scatter | solution.py:147
  149.9 68.3 %reduce-scatter.16.cloned.1.call-start = ((), (), s32[]{:S(2)}) async-start(), calls=%async_computation.14 | async-start | bytes 1769472 | tf_op jit(solution)/shard_map/reduce_scatter | solution.py:151
  153.8 64.5 %copy-start.8 = (bf16[128,768]{1,0:T(8,128)(2,1)S(1)}, bf16[128,768]{1,0:T(8,128)(2,1)}, u32[]{:S(2)}) copy-start(bf16[128,768]{1,0:T(8,128)(2,1)} %param.29) | copy-start | bytes 589828
  153.8 99.4 %reduce-scatter.22.cloned.1.call-start = ((), (), s32[]{:S(2)}) async-start(), calls=%async_computation.18 | async-start | bytes 1327104 | tf_op jit(solution)/shard_map/reduce_scatter | solution.py:188
  222.2 57.7 %reduce-scatter.24.cloned.1.call-start = ((), (), s32[]{:S(2)}) async-start(), calls=%async_computation.19 | async-start | bytes 737280 | tf_op jit(solution)/shard_map/reduce_scatter | solution.py:165
  225.6 100.5 %reduce-scatter.20.cloned.1.call-start = ((), (), s32[]{:S(2)}) async-start(), calls=%async_computation.17 | async-start | bytes 3981312 | tf_op jit(solution)/shard_map/reduce_scatter | solution.py:189
  233.3 4.7 %copy-start.14 = (f32[768]{0:T(1024)S(1)}, f32[768]{0:T(1024)}, u32[]{:S(2)}) copy-start(f32[768]{0:T(1024)} %get-tuple-element.34) | copy-start | bytes 9220
  233.3 119.7 %reduce-scatter.26.cloned.1.call-start = ((), (), s32[]{:S(2)}) async-start(), calls=%async_computation.20 | async-start | bytes 737280 | tf_op jit(solution)/shard_map/reduce_scatter | solution.py:161
  237.9 148.2 %reduce-scatter.28.cloned.1.call-start = ((), (), s32[]{:S(2)}) async-start(), calls=%async_computation.21 | async-start | bytes 442368
  241.5 43.0 %copy-start.18 = (f32[384]{0:T(512)S(1)}, f32[384]{0:T(512)}, u32[]{:S(2)}) copy-start(f32[384]{0:T(512)} %get-tuple-element.32) | copy-start | bytes 4612
  243.0 167.2 %reduce-scatter.32.cloned.1.call-start = ((), (), s32[]{:S(2)}) async-start(), calls=%async_computation.23 | async-start | bytes 184320
  279.9 84.5 %all-to-all-start.1 = ((bf16[8,24,384]{2,1,0:T(8,128)(2,1)}), bf16[8,24,384]{2,1,0:T(8,128)(2,1)S(1)}, u32[]{:S(2)}, u32[]{:S(2)}) async-start(bf16[8,24,384]{2,1,0:T(8,128)(2,1)} %bitcast.117), calls=%async_computation.6 | async-start | bytes 294912 | tf_op jit(solution)/shard_map/all_to_all | solution.py:166
  284.5 152.9 %reduce-scatter.30.cloned.1.call-start = ((), (), s32[]{:S(2)}) async-start(), calls=%async_computation.22 | async-start | bytes 552960
  (15 other events, 33.8 us)
Sparse Core Ops, SparseCore 0:
  9.7 44.2 all-gather.5
  55.6 21.4 all-gather.7
  78.8 36.4 all-gather.11
  117.4 23.8 all-gather.9
  150.0 33.8 reduce-scatter.17
  186.1 32.1 reduce-scatter.15
  222.3 30.8 reduce-scatter.21
  256.7 23.1 reduce-scatter.23
  282.3 43.7 reduce-scatter.19
  329.4 23.5 reduce-scatter.25
  355.4 30.6 reduce-scatter.27
  388.7 21.4 reduce-scatter.31
  413.1 24.2 reduce-scatter.29
where the time goes:
time: 456 us; the launch traced here: 455 us
  waiting for transfers between devices  305 us (67%)
  blocking collectives  63.8 us (14%)
  matrix products  36.5 us (8%)
  other arithmetic  15.5 us (3%)
  between operations  14.5 us (3%)
  local copies, waits for them, and re-layouts  10.1 us (2%)
  starting transfers between devices  8.85 us (2%)
    reduce_scatter x1, waiting for transfers between devices, per_device(): lax.psum_scatter(term_qkv_weight, 'shard', scatter_dimension=0, tiled=True)  41.6 us
    unnamed x16, waiting for transfers between devices  41 us
    all_gather x1, waiting for transfers between devices, per_device(): cot_all = lax.all_gather(cotangent, 'shard', axis=0, tiled=True)  30.8 us
    reduce_scatter x1, waiting for transfers between devices, per_device(): lax.psum_scatter(out_part, 'shard', scatter_dimension=0, tiled=True)  30.8 us
    reduce_scatter x1, waiting for transfers between devices, per_device(): lax.psum_scatter(grad_normed_part, 'shard', scatter_dimension=0, tiled=True)  30.1 us
    reduce_scatter x1, waiting for transfers between devices, per_device(): lax.psum_scatter(term_out_weight, 'rep', scatter_dimension=0, tiled=True)  26.9 us
    reduce_scatter x1, waiting for transfers between devices, per_device(): fc_piece = lax.psum_scatter(fc_rows, 'rep', scatter_dimension=0, tiled=True)  26.6 us
    all_gather x1, waiting for transfers between devices, per_device(): qkv_full = lax.all_gather(qkv_weight, 'shard', axis=0, tiled=True)  26.1 us
  transfers between devices with their start and end apart: 15, of which 13 were waited for; matrix products, arithmetic and copies ran while one was open for 10% of the time, Pallas kernels for 0%

commit v1 on v0

--- a/solution.py
+++ b/solution.py
@@ -115,7 +115,6 @@
     qkv_full = lax.all_gather(qkv_weight, "shard", axis=0, tiled=True)
     proj_full = lax.all_gather(proj_weight, "shard", axis=0, tiled=True)
     fc_cols = lax.all_to_all(fc_weight, "shard", split_axis=1, concat_axis=0, tiled=True)
-    cot_all = lax.all_gather(cotangent, "shard", axis=0, tiled=True)
     inputs = tokens.astype(jnp.float32)
     normed_f, first_back = jax.vjp(layer_norm, inputs, gain_one, shift_one)
     normed_first = normed_f.astype(low)
@@ -131,7 +130,12 @@
     term_out_bias = jnp.sum(cot_f, axis=0) * factor
     normed_s, second_back = jax.vjp(layer_norm, residual, gain_two, shift_two)
     normed_second = normed_s.astype(low)
-    normed_all = lax.all_gather(normed_second, "shard", axis=0, tiled=True)
+    view_the_leaf = lambda xx, obj: jnp.split(
+        lax.all_gather(jnp.concatenate([xx, obj], axis=1), "shard", axis=0, tiled=True),
+        [xx.shape[1]],
+        1,
+    )
+    cot_all, normed_all = view_the_leaf(cotangent, normed_second)
     pre_act = jnp.dot(normed_all, fc_cols, preferred_element_type=jnp.float32) + fc_bias.astype(
         jnp.float32
     )

time: 456 us -> 442 us (0.969)
  waiting for transfers between devices: 305 us -> 295 us
    all_gather x2 -> x1, waiting for transfers between devices: 53.2 us -> 14.9 us  [per_device(): lax.all_gather(jnp.concatenate([xx, obj], axis=1), 'shard', axis=0, tiled...]
    all_to_all x1, waiting for transfers between devices: 0.01 us -> 28.7 us  [per_device(): lax.all_to_all(fc_weight, 'shard', split_axis=1, concat_axis=0, tiled=True)]
    unnamed x16 -> x15, waiting for transfers between devices: 41 us -> 40 us
  transfers between devices with their start and end apart: 15 -> 14, of which waited for: 13 -> 13; matrix products, arithmetic and copies ran while one was open for 10% -> 9% of each run, Pallas kernels for 0% -> 0%
where the time goes in v1:
time: 442 us; the launch traced here: 441 us
  waiting for transfers between devices  295 us (67%)
  blocking collectives  63.8 us (14%)
  matrix products  32.8 us (7%)
  other arithmetic  16.3 us (4%)
  between operations  14.8 us (3%)
  local copies, waits for them, and re-layouts  9.39 us (2%)
  starting transfers between devices  8.83 us (2%)
    reduce_scatter x1, waiting for transfers between devices, per_device(): lax.psum_scatter(term_qkv_weight, 'shard', scatter_dimension=0, tiled=True)  41.6 us
    unnamed x15, waiting for transfers between devices  40 us
    reduce_scatter x1, waiting for transfers between devices, per_device(): lax.psum_scatter(out_part, 'shard', scatter_dimension=0, tiled=True)  30.9 us
    reduce_scatter x1, waiting for transfers between devices, per_device(): lax.psum_scatter(grad_normed_part, 'shard', scatter_dimension=0, tiled=True)  29.2 us
    all_to_all x1, waiting for transfers between devices, per_device(): lax.all_to_all(fc_weight, 'shard', split_axis=1, concat_axis=0, tiled=True)  28.7 us
    reduce_scatter x1, waiting for transfers between devices, per_device(): lax.psum_scatter(term_out_weight, 'rep', scatter_dimension=0, tiled=True)  27 us
    reduce_scatter x1, waiting for transfers between devices, per_device(): fc_piece = lax.psum_scatter(fc_rows, 'rep', scatter_dimension=0, tiled=True)  26.8 us
    all_gather x1, waiting for transfers between devices, per_device(): qkv_full = lax.all_gather(qkv_weight, 'shard', axis=0, tiled=True)  26.3 us
  transfers between devices with their start and end apart: 14, of which 13 were waited for; matrix products, arithmetic and copies ran while one was open for 9% of the time, Pallas kernels for 0%

profile of v1, /device:TPU:0, one launch (start us, length us, event | category | flops | bytes accessed | tf_op | source)
XLA Modules:
  0.0 441.1 jit_solution(860387861600160726)
XLA Ops:
  9.5 14.4 %all-gather = bf16[8,96,8]{1,2,0:T(8,128)(2,1)S(1)} all-gather(bf16[1,96,8]{1,2,0:T(8,128)(2,1)S(1)} %bitcast.116), channel_id=1, replica_groups=mesh['rep'=4,'shard'=8] {'shard'}, dimensions={0}, use_global_device_ids=true | all-gather | bytes 13824 | tf_op jit(solution)/shard_map/all_gather | solution.py:111
  27.6 26.3 %all-gather.5.cloned.1.call-done = bf16[768,2304]{1,0:T(8,128)(2,1)} async-done(((bf16[96,2304]{1,0:T(8,128)(2,1)}), bf16[768,2304]{1,0:T(8,128)(2,1)}) %all-gather.5.cloned.1.call-update) | async-done | bytes 3538960 | tf_op jit(solution)/shard_map/all_gather | solution.py:115
  58.1 19.0 %all-gather.7.cloned.1.call-done = bf16[768,768]{1,0:T(8,128)(2,1)} async-done(((bf16[96,768]{1,0:T(8,128)(2,1)}), bf16[768,768]{1,0:T(8,128)(2,1)}) %all-gather.7.cloned.1.call-update) | async-done | bytes 1179664 | tf_op jit(solution)/shard_map/all_gather | solution.py:116
  81.6 3.5 all-to-all-start
  85.3 28.7 %all-to-all-done = bf16[96,8,384]{2,0,1:T(8,128)(2,1)S(1)} async-done(((bf16[96,8,384]{2,0,1:T(8,128)(2,1)}), bf16[96,8,384]{2,0,1:T(8,128)(2,1)S(1)}, u32[]{:S(2)}, u32[]{:S(2)}) %all-to-all-start) | async-done | bytes 589856 | tf_op jit(solution)/shard_map/all_to_all | solution.py:117
  114.0 14.9 %all-gather.9.cloned.1.call-done = bf16[1024,1536]{1,0:T(8,128)(2,1)} async-done(((bf16[128,1536]{1,0:T(8,128)(2,1)}), bf16[1024,1536]{1,0:T(8,128)(2,1)}) %all-gather.9.cloned.1.call-update) | async-done | bytes 3145744 | tf_op jit(solution)/shard_map/all_gather | solution.py:134
  137.0 3.8 convolution_convert_fusion.1
  140.9 29.2 %reduce-scatter.18.cloned.1.call-done = bf16[128,768]{1,0:T(8,128)(2,1)} async-done(((bf16[1024,768]{1,0:T(8,128)(2,1)}), bf16[128,768]{1,0:T(8,128)(2,1)}) %reduce-scatter.18.cloned.1.call-update) | async-done | bytes 196624 | tf_op jit(solution)/shard_map/reduce_scatter | solution.py:151
  173.7 30.9 %reduce-scatter.16.cloned.1.call-done = bf16[128,768]{1,0:T(8,128)(2,1)} async-done(((bf16[1024,768]{1,0:T(8,128)(2,1)}), bf16[128,768]{1,0:T(8,128)(2,1)}) %reduce-scatter.16.cloned.1.call-update) | async-done | bytes 196624 | tf_op jit(solution)/shard_map/reduce_scatter | solution.py:155
  219.7 3.7 fusion.16
  223.5 3.4 fusion.60
  228.6 10.6 %reduce-scatter.22.cloned.1.call-done = bf16[96,768]{1,0:T(8,128)(2,1)} async-done(((bf16[768,768]{1,0:T(8,128)(2,1)}), bf16[96,768]{1,0:T(8,128)(2,1)}) %reduce-scatter.22.cloned.1.call-update) | async-done | bytes 147472 | tf_op jit(solution)/shard_map/reduce_scatter | solution.py:192
  239.3 26.8 %reduce-scatter.24.cloned.1.call-done = bf16[192,384]{1,0:T(8,128)(2,1)} async-done(((bf16[768,384]{1,0:T(8,128)(2,1)}), bf16[192,384]{1,0:T(8,128)(2,1)}) %reduce-scatter.24.cloned.1.call-update) | async-done | bytes 147472 | tf_op jit(solution)/shard_map/reduce_scatter | solution.py:169
  266.1 4.6 %all-to-all-start.1 = ((bf16[8,24,384]{2,1,0:T(8,128)(2,1)}), bf16[8,24,384]{2,1,0:T(8,128)(2,1)S(1)}, u32[]{:S(2)}, u32[]{:S(2)}) async-start(bf16[8,24,384]{2,1,0:T(8,128)(2,1)} %bitcast.113), calls=%async_computation.6 | async-start | bytes 294912 | tf_op jit(solution)/shard_map/all_to_all | solution.py:170
  270.8 41.6 %reduce-scatter.20.cloned.1.call-done = bf16[96,2304]{1,0:T(8,128)(2,1)} async-done(((bf16[768,2304]{1,0:T(8,128)(2,1)}), bf16[96,2304]{1,0:T(8,128)(2,1)}) %reduce-scatter.20.cloned.1.call-update) | async-done | bytes 442384 | tf_op jit(solution)/shard_map/reduce_scatter | solution.py:193
  312.4 27.0 %reduce-scatter.26.cloned.1.call-done = bf16[96,768]{1,0:T(8,128)(2,1)} async-done(((bf16[384,768]{1,0:T(8,128)(2,1)}), bf16[96,768]{1,0:T(8,128)(2,1)}) %reduce-scatter.26.cloned.1.call-update) | async-done | bytes 147472 | tf_op jit(solution)/shard_map/reduce_scatter | solution.py:165
  339.4 10.2 %all_gather.31 = bf16[384,768]{1,0:T(8,128)(2,1)S(1)} all-gather(bf16[96,768]{1,0:T(8,128)(2,1)} %reduce-scatter.26.cloned.1.call-done), channel_id=1, replica_groups=mesh['rep'=4,'shard'=8] {'rep'}, dimensions={0}, use_global_device_ids=true | all-gather | bytes 737280 | tf_op jit(solution)/shard_map/all_gather | solution.py:166
  350.8 10.5 %all_gather.30 = bf16[96,3072]{1,0:T(8,128)(2,1)S(1)} all-gather(bf16[24,3072]{1,0:T(8,128)(2,1)S(1)} %bitcast.112), channel_id=1, replica_groups=mesh['rep'=4,'shard'=8] {'rep'}, dimensions={0}, use_global_device_ids=true | all-gather | bytes 737280 | tf_op jit(solution)/shard_map/all_gather | solution.py:171
  363.3 9.0 %reduce-scatter.28.cloned.1.call-done = f32[96,8]{1,0:T(8,128)} async-done(((f32[768,8]{1,0:T(8,128)}), f32[96,8]{1,0:T(8,128)}) %reduce-scatter.28.cloned.1.call-update) | async-done | bytes 3088
  373.2 10.6 %all-reduce.2 = (f32[8,96]{1,0:T(8,128)S(1)}, f32[384]{0:T(512)}) all-reduce(f32[8,96]{1,0:T(8,128)S(1)} %copy.93, f32[384]{0:T(512)S(1)} %broadcast_multiply_fusion.8), channel_id=1, replica_groups=mesh['rep'=4,'shard'=8] {'rep'}, use_global_device_ids=true, to_apply=%region_21.22 | all-reduce | flops 1152 | bytes 9216 | tf_op jit(solution)/shard_map/psum | solution.py:210
  384.8 11.8 %reduce-scatter.32.cloned.1.call-done = bf16[24,768]{1,0:T(8,128)(2,1)} async-done(((bf16[96,768]{1,0:T(8,128)(2,1)}), bf16[24,768]{1,0:T(8,128)(2,1)}) %reduce-scatter.32.cloned.1.call-update) | async-done | bytes 36880
  396.6 8.5 %all_gather.29 = bf16[96,768]{1,0:T(8,128)(2,1)S(1)} all-gather(bf16[24,768]{1,0:T(8,128)(2,1)} %reduce-scatter.32.cloned.1.call-done), channel_id=1, replica_groups=mesh['rep'=4,'shard'=8] {'rep'}, dimensions={0}, use_global_device_ids=true | all-gather | bytes 184320 | tf_op jit(solution)/shard_map/all_gather | solution.py:196
  405.8 17.7 %reduce-scatter.30.cloned.1.call-done = bf16[24,2304]{1,0:T(8,128)(2,1)} async-done(((bf16[96,2304]{1,0:T(8,128)(2,1)}), bf16[24,2304]{1,0:T(8,128)(2,1)}) %reduce-scatter.30.cloned.1.call-update) | async-done | bytes 110608
  423.6 9.7 %all_gather.28 = bf16[96,2304]{1,0:T(8,128)(2,1)S(1)} all-gather(bf16[24,2304]{1,0:T(8,128)(2,1)} %reduce-scatter.30.cloned.1.call-done), channel_id=1, replica_groups=mesh['rep'=4,'shard'=8] {'rep'}, dimensions={0}, use_global_device_ids=true | all-gather | bytes 552960 | tf_op jit(solution)/shard_map/all_gather | solution.py:197
  (159 shorter events, 49.8 us)
Async XLA Ops:
  7.2 124.2 %copy-start = (bf16[384,768]{1,0:T(8,128)(2,1)S(1)}, bf16[384,768]{1,0:T(8,128)(2,1)}, u32[]{:S(2)}) copy-start(bf16[384,768]{1,0:T(8,128)(2,1)} %param.27) | copy-start | bytes 1769476
  7.2 46.7 %all-gather.5.cloned.1.call-start = ((), (), s32[]{:S(2)}) async-start(), calls=%async_computation.11 | async-start | bytes 3981312 | tf_op jit(solution)/shard_map/all_gather | solution.py:115
  7.9 69.2 %all-gather.7.cloned.1.call-start = ((), (), s32[]{:S(2)}) async-start(), calls=%async_computation.12 | async-start | bytes 1327104 | tf_op jit(solution)/shard_map/all_gather | solution.py:116
  8.7 120.2 %all-gather.9.cloned.1.call-start = ((), (), s32[]{:S(2)}) async-start(), calls=%async_computation.13 | async-start | bytes 3538944 | tf_op jit(solution)/shard_map/all_gather | solution.py:134
  25.0 28.9 %copy-start.10 = (f32[128]{0:T(128)}, f32[128]{0:T(128)S(1)}, u32[]{:S(2)}) copy-start(f32[128]{0:T(128)S(1)} %broadcast_multiply_fusion.10) | copy-start | bytes 1540
  26.8 27.1 %copy-start.23 = (f32[128]{0:T(128)}, f32[128]{0:T(128)S(1)}, u32[]{:S(2)}) copy-start(f32[128]{0:T(128)S(1)} %fusion.37) | copy-start | bytes 1540
  26.8 27.1 %copy-start.18 = (f32[128]{0:T(128)}, f32[128]{0:T(128)S(1)}, u32[]{:S(2)}) copy-start(f32[128]{0:T(128)S(1)} %fusion.51) | copy-start | bytes 1540
  58.1 21.8 %copy-start.7 = (bf16[128,768]{1,0:T(8,128)(2,1)S(1)}, bf16[128,768]{1,0:T(8,128)(2,1)}, u32[]{:S(2)}) copy-start(bf16[128,768]{1,0:T(8,128)(2,1)} %param.29) | copy-start | bytes 589828
  78.9 93.0 %copy-start.17 = (f32[128]{0:T(128)}, f32[128]{0:T(128)S(1)}, u32[]{:S(2)}) copy-start(f32[128]{0:T(128)S(1)} %broadcast_multiply_fusion.9) | copy-start | bytes 1540
  79.1 92.8 %copy-start.20 = (f32[128]{0:T(128)}, f32[128]{0:T(128)S(1)}, u32[]{:S(2)}) copy-start(f32[128]{0:T(128)S(1)} %fusion.52) | copy-start | bytes 1540
  81.6 32.3 %all-to-all-start = ((bf16[96,8,384]{2,0,1:T(8,128)(2,1)}), bf16[96,8,384]{2,0,1:T(8,128)(2,1)S(1)}, u32[]{:S(2)}, u32[]{:S(2)}) async-start(bf16[96,8,384]{2,0,1:T(8,128)(2,1)} %bitcast.87), calls=%async_computation | async-start | bytes 1179648 | tf_op jit(solution)/shard_map/all_to_all | solution.py:117
  85.2 84.9 %reduce-scatter.18.cloned.1.call-start = ((), (), s32[]{:S(2)}) async-start(), calls=%async_computation.15 | async-start | bytes 1769472 | tf_op jit(solution)/shard_map/reduce_scatter | solution.py:151
  136.9 67.6 %reduce-scatter.16.cloned.1.call-start = ((), (), s32[]{:S(2)}) async-start(), calls=%async_computation.14 | async-start | bytes 1769472 | tf_op jit(solution)/shard_map/reduce_scatter | solution.py:155
  140.8 29.3 %copy-start.9 = (f32[768]{0:T(1024)S(1)}, f32[768]{0:T(1024)}, u32[]{:S(2)}) copy-start(f32[768]{0:T(1024)} %get-tuple-element.24) | copy-start | bytes 9220
  140.8 63.8 %copy-start.12 = (f32[768]{0:T(1024)S(1)}, f32[768]{0:T(1024)}, u32[]{:S(2)}) copy-start(f32[768]{0:T(1024)} %get-tuple-element.22) | copy-start | bytes 9220
  140.8 98.5 %reduce-scatter.22.cloned.1.call-start = ((), (), s32[]{:S(2)}) async-start(), calls=%async_computation.17 | async-start | bytes 1327104 | tf_op jit(solution)/shard_map/reduce_scatter | solution.py:192
  208.6 57.5 %reduce-scatter.24.cloned.1.call-start = ((), (), s32[]{:S(2)}) async-start(), calls=%async_computation.18 | async-start | bytes 737280 | tf_op jit(solution)/shard_map/reduce_scatter | solution.py:169
  212.0 100.4 %reduce-scatter.20.cloned.1.call-start = ((), (), s32[]{:S(2)}) async-start(), calls=%async_computation.16 | async-start | bytes 3981312 | tf_op jit(solution)/shard_map/reduce_scatter | solution.py:193
  219.7 119.8 %reduce-scatter.26.cloned.1.call-start = ((), (), s32[]{:S(2)}) async-start(), calls=%async_computation.19 | async-start | bytes 737280 | tf_op jit(solution)/shard_map/reduce_scatter | solution.py:165
  223.5 148.8 %reduce-scatter.28.cloned.1.call-start = ((), (), s32[]{:S(2)}) async-start(), calls=%async_computation.20 | async-start | bytes 442368
  227.0 43.8 %copy-start.21 = (f32[384]{0:T(512)S(1)}, f32[384]{0:T(512)}, u32[]{:S(2)}) copy-start(f32[384]{0:T(512)} %get-tuple-element.55) | copy-start | bytes 4612
  228.6 168.0 %reduce-scatter.32.cloned.1.call-start = ((), (), s32[]{:S(2)}) async-start(), calls=%async_computation.22 | async-start | bytes 184320
  266.1 84.7 %all-to-all-start.1 = ((bf16[8,24,384]{2,1,0:T(8,128)(2,1)}), bf16[8,24,384]{2,1,0:T(8,128)(2,1)S(1)}, u32[]{:S(2)}, u32[]{:S(2)}) async-start(bf16[8,24,384]{2,1,0:T(8,128)(2,1)} %bitcast.113), calls=%async_computation.6 | async-start | bytes 294912 | tf_op jit(solution)/shard_map/all_to_all | solution.py:170
  270.7 152.9 %reduce-scatter.30.cloned.1.call-start = ((), (), s32[]{:S(2)}) async-start(), calls=%async_computation.21 | async-start | bytes 552960
  (19 other events, 62.6 us)
Sparse Core Ops, SparseCore 0:
  9.7 44.2 all-gather.4
  55.6 21.5 all-gather.6
  80.9 47.9 all-gather.8
  137.0 32.9 reduce-scatter.17
  172.2 32.2 reduce-scatter.15
  208.7 30.5 reduce-scatter.21
  242.7 23.3 reduce-scatter.23
  268.5 43.8 reduce-scatter.19
  315.8 23.5 reduce-scatter.25
  341.6 30.6 reduce-scatter.27
  375.1 21.4 reduce-scatter.31
  399.3 24.2 reduce-scatter.29
